TPU v7x, 128 devices: a whole 4x4x4 slice. The times are simulated.
128 devices in a mesh: sec: 2 (over y_lo), dp: 16 (over z, y_hi, core), tensor: 4 (over x).
Axes of the slice: x: 4, y: 4 (y_hi: 2, y_lo: 2; y = y_hi * 2 + y_lo), z: 4, core: 2. Of those that a mesh axis runs over, the one named last changes fastest.
Arguments:
- student_rows: bfloat16 [2, 8192, 5376], P('sec', 'dp'), may hold values from -24 to 24
- teacher_rows: bfloat16 [2, 8192, 5376], P('sec', 'dp'), may hold values from -6 to 6
- norm_gain: float32 [5376], replicated, may hold values from 0.5 to 1.5
- post_gain: float32 [5376], replicated, may hold values from 0.5 to 1.5
- query_weight: bfloat16 [5376, 2048], P(('sec', 'dp'), 'tensor')
- key_weight: bfloat16 [5376, 1024], P(('sec', 'dp'), 'tensor')
- value_weight: bfloat16 [5376, 1024], P(('sec', 'dp'), 'tensor'), may hold values from -0.078125 to 0.078125
- out_weight: bfloat16 [5376, 2048], P(('sec', 'dp'), 'tensor'), may hold values from -0.125 to 0.125
Outputs:
- layer_output: bfloat16 [2, 8192, 5376], P('sec', 'dp', 'tensor')
- query_grad: float32 [5376, 2048], P(('sec', 'dp'), 'tensor')
- output_grad: float32 [5376, 2048], P(('sec', 'dp'), 'tensor')
All inputs are finite; a program needn't handle non-finite values.
Results may differ from a plain program's by a relative error of at most 0.025.
The roundings to bfloat16 on the way count: a program that leaves them out, or rounds other values in their place, can miss the bound.
Values may be sent and summed in bfloat16 or wider, within the bound.
A program may use at most 128 MiB of HBM per device.

v0:
```python
import math
import jax
import jax.numpy as jnp
from jax import lax
from jax.sharding import PartitionSpec as P

HEADS = 8
KV_HEADS = 4
HD = 256
W = 1024
norm_eps = 1e-06
rope_base = 10000.0
masked_score = -1e30


def from_partner(block, axis, bit):
    count = lax.axis_size(axis)
    route = []
    for low in range(count):
        high = low | 1 << bit
        if high != low and high < count:
            route += [(low, high), (high, low)]
    return lax.ppermute(block, axis, route)


def from_behind(x, axis, by):
    count = lax.axis_size(axis)
    pairs = [(i, i + by) for i in range(count) if 0 <= i + by < count]
    return lax.ppermute(x, axis, pairs)


def rotate(values, cos_table, sin_table, sign_value):
    row_count = values.shape[0]
    half_dim = cos_table.shape[1]
    per_head = values.reshape(row_count, -1, 2 * half_dim)
    leading = per_head[:, :, :half_dim]
    trailing = per_head[:, :, half_dim:]
    cosines = cos_table[:, None, :]
    sin_scaled = sign_value * sin_table[:, None, :]
    rotated = jnp.concatenate(
        [leading * cosines - trailing * sin_scaled, trailing * cosines + leading * sin_scaled],
        axis=2,
    )
    return rotated.reshape(row_count, -1)


def shards(
    student_rows,
    teacher_rows,
    norm_gain,
    post_gain,
    query_weight,
    key_weight,
    value_weight,
    out_weight,
):
    tok_count = student_rows.shape[1]
    model_width = student_rows.shape[2]
    tensor_count = lax.axis_size("tensor")
    share_cols = model_width // tensor_count
    data_count = lax.axis_size("sec") * lax.axis_size("dp")
    blocks_back = (W + tok_count - 1) // tok_count
    key_count = (blocks_back + 1) * tok_count
    local_groups = key_weight.shape[1] // HD
    group_size = HEADS // KV_HEADS
    query_cols = query_weight.shape[1]
    score_scale = 1.0 / math.sqrt(HD)
    loss_scale = 2.0 / math.sqrt(data_count * tok_count)
    target = from_partner(teacher_rows[0], "sec", 0)
    query_full, key_full, value_full, out_full = (
        lax.all_gather(query_weight, ("sec", "dp"), axis=0, tiled=True),
        lax.all_gather(key_weight, ("sec", "dp"), axis=0, tiled=True),
        lax.all_gather(value_weight, ("sec", "dp"), axis=0, tiled=True),
        lax.all_gather(out_weight, ("sec", "dp"), axis=0, tiled=True),
    )
    student_f = student_rows[0].astype(jnp.float32)
    inverse = lax.rsqrt(jnp.mean(student_f * student_f, axis=1, keepdims=True) + norm_eps)
    normed = (student_f * inverse * norm_gain).astype(jnp.bfloat16)
    first_pos = lax.axis_index("dp") * tok_count
    half_dim = HD // 2
    inv_freq = jnp.power(
        jnp.float32(rope_base), -2.0 * jnp.arange(half_dim, dtype=jnp.float32) / HD
    )
    positions = (first_pos + jnp.arange(tok_count, dtype=jnp.int32)).astype(jnp.float32)
    angles = positions[:, None] * inv_freq[None, :]
    cos_table = jnp.cos(angles)
    sin_table = jnp.sin(angles)
    queries = rotate(
        jnp.dot(normed, query_full, preferred_element_type=jnp.float32), cos_table, sin_table, 1.0
    ).astype(jnp.bfloat16)
    key_rows = rotate(
        jnp.dot(normed, key_full, preferred_element_type=jnp.float32), cos_table, sin_table, 1.0
    ).astype(jnp.bfloat16)
    value_rows = jnp.dot(normed, value_full, preferred_element_type=jnp.float32).astype(
        jnp.bfloat16
    )
    key_parts = [key_rows]
    value_parts = [value_rows]
    for offset in range(1, blocks_back + 1):
        earlier_keys, earlier_values = from_behind((key_rows, value_rows), "dp", offset)
        key_parts = [earlier_keys] + key_parts
        value_parts = [earlier_values] + value_parts
    key_window = jnp.concatenate(key_parts, axis=0)
    value_window = jnp.concatenate(value_parts, axis=0)
    query_pos = first_pos + jnp.arange(tok_count, dtype=jnp.int32)
    key_pos = first_pos - blocks_back * tok_count + jnp.arange(key_count, dtype=jnp.int32)
    allowed = (
        (key_pos[None, :] >= 0)
        & (key_pos[None, :] <= query_pos[:, None])
        & (key_pos[None, :] > query_pos[:, None] - W)
    )
    grouped_q = queries.reshape(tok_count, local_groups, group_size, HD)
    grouped_k = key_window.reshape(key_count, local_groups, HD)
    grouped_v = value_window.reshape(key_count, local_groups, HD)
    scores = (
        jnp.einsum("tgad,kgd->gatk", grouped_q, grouped_k, preferred_element_type=jnp.float32)
        * score_scale
    )
    scores = jnp.where(allowed, scores, masked_score)
    row_peak = jnp.max(scores, axis=3, keepdims=True)
    exp_scores = jnp.exp(scores - row_peak)
    attn_probs = exp_scores / jnp.sum(exp_scores, axis=3, keepdims=True)
    probs_b = attn_probs.astype(jnp.bfloat16)
    mixed_rows = (
        jnp.einsum("gatk,kgd->tgad", probs_b, grouped_v, preferred_element_type=jnp.float32)
        .astype(jnp.bfloat16)
        .reshape(tok_count, query_cols)
    )
    partial_value = jnp.einsum(
        "te,de->td", mixed_rows, out_full, preferred_element_type=jnp.float32
    )
    summed = lax.psum(partial_value.astype(jnp.bfloat16), "tensor").astype(jnp.float32)
    post_factor = lax.rsqrt(jnp.mean(summed * summed, axis=1, keepdims=True) + norm_eps)
    layer_full = (student_f + summed * post_factor * post_gain).astype(jnp.bfloat16)
    loss_grad = loss_scale * (layer_full.astype(jnp.float32) - target.astype(jnp.float32))
    scaled = post_gain * loss_grad
    along_sum = jnp.mean(summed * scaled, axis=1, keepdims=True)
    pre_grad = (
        post_factor * scaled - summed * post_factor * post_factor * post_factor * along_sum
    ).astype(jnp.bfloat16)
    mixed_grad = jnp.dot(pre_grad, out_full, preferred_element_type=jnp.float32).astype(
        jnp.bfloat16
    )
    grouped_g = mixed_grad.reshape(tok_count, local_groups, group_size, HD)
    prob_grad = jnp.einsum(
        "tgad,kgd->gatk", grouped_g, grouped_v, preferred_element_type=jnp.float32
    )
    score_grad = (
        attn_probs * (prob_grad - jnp.sum(attn_probs * prob_grad, axis=3, keepdims=True))
    ).astype(jnp.bfloat16)
    rotated_grad = (
        jnp.einsum(
            "gatk,kgd->tgad", score_grad, grouped_k, preferred_element_type=jnp.float32
        ).reshape(tok_count, query_cols)
        * score_scale
    )
    query_pre = rotate(rotated_grad, cos_table, sin_table, -1.0).astype(jnp.bfloat16)
    query_term = jnp.einsum("td,te->de", normed, query_pre, preferred_element_type=jnp.float32)
    out_term = jnp.einsum("td,te->de", pre_grad, mixed_rows, preferred_element_type=jnp.float32)
    grad_owned = lax.psum_scatter(
        jnp.concatenate([query_term, out_term], axis=1).astype(jnp.bfloat16),
        ("sec", "dp"),
        scatter_dimension=0,
        tiled=True,
    ).astype(jnp.float32)
    layer_share = lax.dynamic_slice_in_dim(
        layer_full, lax.axis_index("tensor") * share_cols, share_cols, 1
    )
    return (layer_share[None], grad_owned[:, :query_cols], grad_owned[:, query_cols:])


def solution(mesh):
    in_specs = (
        P("sec", "dp", None),
        P("sec", "dp", None),
        P(),
        P(),
        P(("sec", "dp"), "tensor"),
        P(("sec", "dp"), "tensor"),
        P(("sec", "dp"), "tensor"),
        P(("sec", "dp"), "tensor"),
    )
    out_specs = (P("sec", "dp", "tensor"), P(("sec", "dp"), "tensor"), P(("sec", "dp"), "tensor"))
    return jax.shard_map(shards, mesh=mesh, in_specs=in_specs, out_specs=out_specs, check_vma=False)
```

profile of v0, /device:TPU:2, one launch (start us, length us, event | category | flops | bytes accessed | tf_op | source)
XLA Modules:
  0.0 628.8 jit_solution(17924069632204809534)
XLA Ops:
  7.2 0.7 all-gather.7.cloned.1.call-update
  8.0 0.7 all-gather.5.cloned.1.call-update
  8.7 0.7 all-gather.9.cloned.1.call-update
  9.4 0.5 all-gather.11.cloned.1.call-update
  10.1 3.7 fusion.9
  13.8 1.0 broadcast_multiply_fusion
  14.8 1.2 compare_and_fusion
  16.0 53.6 %all-gather.7.cloned.1.call-done = bf16[5376,256]{1,0:T(8,128)(2,1)} async-done(((bf16[168,256]{1,0:T(8,128)(2,1)}), bf16[5376,256]{1,0:T(8,128)(2,1)}) %all-gather.7.cloned.1.call-update) | async-done | bytes 2752528 | tf_op jit(solution)/shard_map/all_gather | solution.py:72
  69.6 5.4 fusion.50
  75.0 1.2 fusion.66
  76.2 2.1 collective-permute-start.3
  78.4 4.0 collective-permute-start.2
  82.4 53.2 %all-gather.5.cloned.1.call-done = bf16[5376,256]{1,0:T(8,128)(2,1)} async-done(((bf16[168,256]{1,0:T(8,128)(2,1)}), bf16[5376,256]{1,0:T(8,128)(2,1)}) %all-gather.5.cloned.1.call-update) | async-done | bytes 2752528 | tf_op jit(solution)/shard_map/all_gather | solution.py:73
  135.6 5.0 fusion.53
  140.7 2.1 collective-permute-start.1
  142.8 4.3 collective-permute-start
  147.1 57.4 %all-gather.9.cloned.1.call-done = bf16[5376,512]{1,0:T(8,128)(2,1)} async-done(((bf16[168,512]{1,0:T(8,128)(2,1)}), bf16[5376,512]{1,0:T(8,128)(2,1)}) %all-gather.9.cloned.1.call-update) | async-done | bytes 5505040 | tf_op jit(solution)/shard_map/all_gather | solution.py:71
  204.5 8.3 %copy.30 = bf16[512,5376]{1,0:T(8,128)(2,1)} copy(bf16[512,5376]{0,1:T(8,128)(2,1)} %bitcast.134) | data formatting | bytes 11010048 | tf_op jit(solution)/shard_map/dot_general | solution.py:89
  212.8 7.0 %fusion.22 = f32[512,2,256]{0,2,1:T(8,128)S(1)} fusion(bf16[2,256,5376]{2,1,0:T(8,128)(2,1)} %bitcast.135, bf16[1,512,5376]{2,1,0:T(8,128)(2,1)} %param.8, f32[5376]{0:T(1024)S(1)} %copy-done.4, f32[512]{0:T(512)S(1)} %add_rsqrt_fusion.1), kind=kOutput, calls=%fused_computation.36 | convolution fusion | flops 2829582336 | bytes 12082176 | tf_op jit(solution)/shard_map/dot_general | solution.py:89
  219.7 0.2 subtract_convert_fusion.1
  220.0 1.4 fusion.25
  221.4 1.5 fusion.21
  222.9 1.1 copy-done.2
  224.0 3.1 fusion.47
  227.1 39.8 %all-gather.11.cloned.1.call-done = bf16[5376,512]{1,0:T(8,128)(2,1)} async-done(((bf16[168,512]{1,0:T(8,128)(2,1)}), bf16[5376,512]{1,0:T(8,128)(2,1)}) %all-gather.11.cloned.1.call-update) | async-done | bytes 5505040 | tf_op jit(solution)/shard_map/all_gather | solution.py:74
  266.9 8.3 %convolution_convert_fusion.2 = bf16[512,5376]{1,0:T(8,128)(2,1)} fusion(bf16[512,512]{0,1:T(8,128)(2,1)} %bitcast.139, bf16[5376,512]{1,0:T(8,128)(2,1)} %all-gather.11.cloned.1.call-done), kind=kOutput, calls=%fused_computation.26 | convolution fusion | flops 2821324800 | bytes 11534336 | tf_op jit(solution)/shard_map/te,de->td/dot_general | solution.py:129
  275.2 0.0 reduce-scatter.4.cloned.1.call-start
  275.3 1.6 collective-permute-start.4
  276.8 110.7 %all-reduce.2.cloned.1.call-done = bf16[512,5376]{1,0:T(8,128)(2,1)} async-done(((bf16[512,5376]{1,0:T(8,128)(2,1)}), bf16[512,5376]{1,0:T(8,128)(2,1)}) %all-reduce.2.cloned.1.call-update) | async-done | bytes 5505040 | tf_op jit(solution)/shard_map/psum | solution.py:132
  387.5 3.9 fusion.15
  391.4 5.3 collective-permute-done.4
  396.7 7.1 %fusion.16 = (f32[512]{0:T(512)S(1)}, bf16[512,5376]{1,0:T(8,128)(2,1)S(1)}) fusion(bf16[512,5376]{1,0:T(8,128)(2,1)S(1)} %copy-done, bf16[512,5376]{1,0:T(8,128)(2,1)} %collective-permute-done.4, f32[5376]{0:T(1024)S(1)} %broadcast_multiply_fusion.1, f32[5376]{0:T(1024)S(1)} %copy-done.3, f32[512]{0:T(512)S(1)} %add_rsqrt_fusion, bf16[1,512,5376]{2,1,0:T(8,128)(2,1)} %param.8), kind=kLoop, calls=%fused_computation.21 | loop fusion | flops 33029632 | bytes 22067200 | tf_op jit(solution)/shard_map/reduce_sum | solution.py:137
  403.8 8.0 %fusion.8 = bf16[512,5376]{1,0:T(8,128)(2,1)S(1)} fusion(bf16[512,5376]{1,0:T(8,128)(2,1)S(1)} %copy-done, bf16[512,5376]{1,0:T(8,128)(2,1)} %collective-permute-done.4, bf16[512,5376]{1,0:T(8,128)(2,1)S(1)} %get-tuple-element.13, f32[512]{0:T(512)S(1)} %broadcast_multiply_fusion.2, f32[5376]{0:T(1024)S(1)} %broadcast_multiply_fusion.1, f32[512]{0:T(512)S(1)} %add_rsqrt_fusion), kind=kLoop, calls=%fused_computation.13 | loop fusion | flops 33030144 | bytes 22045696 | tf_op jit(solution)/shard_map/convert_element_type | solution.py:140
  411.8 3.2 convolution_convert_fusion
  415.1 5.8 convolution_convert_fusion.3
  420.9 2.3 fusion.17
  423.2 2.7 fusion.44
  425.9 0.2 subtract_convert_fusion
  426.2 3.6 convolution_convert_fusion.1
  429.9 5.1 pad_maximum_fusion
  435.0 14.7 %copy.48 = bf16[5376,1024]{1,0:T(8,128)(2,1)} copy(bf16[5376,1024]{0,1:T(8,128)(2,1)} %pad_maximum_fusion) | data formatting | bytes 22020096
  449.7 2.3 constant_dynamic-slice_fusion
  452.0 1.5 copy.35
  453.5 165.0 %reduce-scatter.4.cloned.1.call-done = bf16[168,1024]{1,0:T(8,128)(2,1)} async-done(((bf16[5376,1024]{1,0:T(8,128)(2,1)}), bf16[168,1024]{1,0:T(8,128)(2,1)}) %reduce-scatter.4.cloned.1.call-update) | async-done | bytes 344080
  618.4 1.2 copy.49
  619.6 0.1 fusion.80
  619.7 0.9 copy.39
  620.6 0.9 copy.38
  (43 shorter events, 0.4 us)
Async XLA Ops:
  7.2 62.5 %copy-start.4 = (f32[5376]{0:T(1024)S(1)}, f32[5376]{0:T(1024)}, u32[]{:S(2)}) copy-start(f32[5376]{0:T(1024)} %param.10) | copy-start | bytes 64516
  7.2 62.5 %all-gather.7.cloned.1.call-start = ((), (), s32[]{:S(2)}) async-start(), calls=%async_computation.2 | async-start | bytes 2838528 | tf_op jit(solution)/shard_map/all_gather | solution.py:72
  7.9 127.7 %all-gather.5.cloned.1.call-start = ((), (), s32[]{:S(2)}) async-start(), calls=%async_computation.1 | async-start | bytes 2838528 | tf_op jit(solution)/shard_map/all_gather | solution.py:73
  8.7 195.8 %all-gather.9.cloned.1.call-start = ((), (), s32[]{:S(2)}) async-start(), calls=%async_computation.3 | async-start | bytes 5677056 | tf_op jit(solution)/shard_map/all_gather | solution.py:71
  9.4 257.5 %all-gather.11.cloned.1.call-start = ((), (), s32[]{:S(2)}) async-start(), calls=%async_computation.4 | async-start | bytes 5677056 | tf_op jit(solution)/shard_map/all_gather | solution.py:74
  10.0 377.5 %all-reduce.2.cloned.1.call-start = ((), (), s32[]{:S(2)}) async-start(), calls=%async_computation.5 | async-start | bytes 11010048 | tf_op jit(solution)/shard_map/psum | solution.py:132
  76.2 143.7 %collective-permute-start.3 = (bf16[512,256]{0,1:T(8,128)(2,1)S(1)}, bf16[512,256]{0,1:T(8,128)(2,1)S(1)}, u32[]{:S(2)}, u32[]{:S(2)}) collective-permute-start(bf16[512,256]{0,1:T(8,128)(2,1)S(1)} %maximum_bitcast_fusion.6), channel_id=1, source_target_pairs={{0,4},{4,8},{8,12},{12,16},{16,20},{20,24},{24,28},{28,32},{32,36}... | collective-permute-start | bytes 786440 | tf_op jit(solution)/shard_map/ppermute | solution.py:29
  78.4 141.6 %collective-permute-start.2 = (bf16[512,256]{0,1:T(8,128)(2,1)S(1)}, bf16[512,256]{0,1:T(8,128)(2,1)S(1)}, u32[]{:S(2)}, u32[]{:S(2)}) collective-permute-start(bf16[512,256]{0,1:T(8,128)(2,1)S(1)} %maximum_bitcast_fusion.6), channel_id=1, source_target_pairs={{0,8},{4,12},{8,16},{12,20},{16,24},{20,28},{24,32},{28,36},{32,40... | collective-permute-start | bytes 786440 | tf_op jit(solution)/shard_map/ppermute | solution.py:29
  140.7 82.2 %collective-permute-start.1 = (bf16[512,256]{1,0:T(8,128)(2,1)S(1)}, bf16[512,256]{1,0:T(8,128)(2,1)S(1)}, u32[]{:S(2)}, u32[]{:S(2)}) collective-permute-start(bf16[512,256]{1,0:T(8,128)(2,1)S(1)} %fusion.53), channel_id=1, source_target_pairs={{0,4},{4,8},{8,12},{12,16},{16,20},{20,24},{24,28},{28,32},{32,36}... | collective-permute-start | bytes 786440 | tf_op jit(solution)/shard_map/ppermute | solution.py:29
  142.8 80.1 %collective-permute-start = (bf16[512,256]{1,0:T(8,128)(2,1)S(1)}, bf16[512,256]{1,0:T(8,128)(2,1)S(1)}, u32[]{:S(2)}, u32[]{:S(2)}) collective-permute-start(bf16[512,256]{1,0:T(8,128)(2,1)S(1)} %fusion.53), channel_id=1, source_target_pairs={{0,8},{4,12},{8,16},{12,20},{16,24},{20,28},{24,32},{28,36},{32,40... | collective-permute-start | bytes 786440 | tf_op jit(solution)/shard_map/ppermute | solution.py:29
  221.4 2.7 copy-start.2
  266.9 9.9 %copy-start.3 = (f32[5376]{0:T(1024)S(1)}, f32[5376]{0:T(1024)}, u32[]{:S(2)}) copy-start(f32[5376]{0:T(1024)} %param.11) | copy-start | bytes 64516
  275.2 343.2 %reduce-scatter.4.cloned.1.call-start = ((), (), s32[]{:S(2)}) async-start(), calls=%async_computation.6 | async-start | bytes 11354112
  275.3 121.4 %collective-permute-start.4 = (bf16[512,5376]{1,0:T(8,128)(2,1)}, bf16[512,5376]{1,0:T(8,128)(2,1)}, u32[]{:S(2)}, u32[]{:S(2)}) collective-permute-start(bf16[512,5376]{1,0:T(8,128)(2,1)} %bitcast.138), channel_id=1, source_target_pairs={{0,64},{64,0},{1,65},{65,1},{2,66},{66,2},{3,67},{67,3},{4,68},{68... | collective-permute-start | bytes 16515080 | tf_op jit(solution)/shard_map/ppermute | solution.py:23
  387.5 9.2 %copy-start = (bf16[512,5376]{1,0:T(8,128)(2,1)S(1)}, bf16[512,5376]{1,0:T(8,128)(2,1)}, u32[]{:S(2)}) copy-start(bf16[512,5376]{1,0:T(8,128)(2,1)} %all-reduce.2.cloned.1.call-done) | copy-start | bytes 16515076
  403.8 8.0 %copy-start.1 = (bf16[512,5376]{1,0:T(8,128)(2,1)}, bf16[512,5376]{1,0:T(8,128)(2,1)S(1)}, u32[]{:S(2)}) copy-start(bf16[512,5376]{1,0:T(8,128)(2,1)S(1)} %get-tuple-element.13) | copy-start | bytes 16515076
  403.8 8.0 %copy-start.5 = (bf16[256,2,512]{2,0,1:T(8,128)(2,1)S(1)}, bf16[256,2,512]{2,0,1:T(8,128)(2,1)}, u32[]{:S(2)}) copy-start(bf16[256,2,512]{2,0,1:T(8,128)(2,1)} %fusion.47) | copy-start | bytes 1572868
  411.8 9.0 %slice-start.2 = ((s8[6291456]{0:T(1024)(128)(4,1)}), s8[4194304]{0:T(1024)(128)(4,1)S(1)}, s32[]{:S(2)}) async-start(s8[6291456]{0:T(1024)(128)(4,1)} %bitcast.132), calls=%async_computation.9 | async-start | bytes 8388608
  415.1 5.8 slice-start.3
  420.9 5.4 slice-start
  423.2 3.0 slice-start.1
Sparse Core Ops, SparseCore 0:
  9.7 59.8 all-gather.6
  71.3 64.2 all-gather.4
  137.3 67.1 all-gather.8
  206.1 60.8 all-gather.10
  275.3 112.1 all-reduce.1
  449.8 168.6 reduce-scatter.3
where the time goes:
time: 635 us; the launch traced here: 629 us
  waiting for transfers between devices  488 us (77%)
  matrix products  47.8 us (8%)
  other arithmetic  33.1 us (5%)
  local copies, waits for them, and re-layouts  31 us (5%)
  between operations  14.9 us (2%)
  starting transfers between devices  14.3 us (2%)
    unnamed x7, waiting for transfers between devices  168 us
    psum x1, waiting for transfers between devices, shards(): lax.psum(partial_value.astype(jnp.bfloat16), 'tensor').astype(jnp.float32)  111 us
    all_gather x1, waiting for transfers between devices, shards(): lax.all_gather(query_weight, ('sec', 'dp'), axis=0, tiled=True)  57.4 us
    all_gather x1, waiting for transfers between devices, shards(): lax.all_gather(key_weight, ('sec', 'dp'), axis=0, tiled=True)  53.6 us
    all_gather x1, waiting for transfers between devices, shards(): lax.all_gather(value_weight, ('sec', 'dp'), axis=0, tiled=True)  53.2 us
    all_gather x1, waiting for transfers between devices, shards(): lax.all_gather(out_weight, ('sec', 'dp'), axis=0, tiled=True)  39.8 us
    unnamed x24, local copies, waits for them, and re-layouts  18.9 us
  transfers between devices with their start and end apart: 11, of which 7 were waited for; matrix products, arithmetic and copies ran while one was open for 7% of the time, Pallas kernels for 0%

commit v1 on v0

--- a/solution.py
+++ b/solution.py
@@ -69,7 +69,12 @@
     target = from_partner(teacher_rows[0], "sec", 0)
     query_full, key_full, value_full, out_full = (
         lax.all_gather(query_weight, ("sec", "dp"), axis=0, tiled=True),
-        lax.all_gather(key_weight, ("sec", "dp"), axis=0, tiled=True),
+        jnp.concatenate(
+            lax.all_to_all(
+                jnp.stack([key_weight] * lax.axis_size(("sec", "dp"))), ("sec", "dp"), 0, 0
+            ),
+            axis=0,
+        ),
         lax.all_gather(value_weight, ("sec", "dp"), axis=0, tiled=True),
         lax.all_gather(out_weight, ("sec", "dp"), axis=0, tiled=True),
     )

time: 635 us -> 590 us (0.929)
  waiting for transfers between devices: 488 us -> 439 us
  starting transfers between devices: 14.3 us -> 22.2 us
    all_gather x1 -> x0, waiting for transfers between devices: 53.6 us -> none  [shards(): lax.all_gather(key_weight, ('sec', 'dp'), axis=0, tiled=True)]
    all_to_all x0 -> x1, waiting for transfers between devices: none -> 31.8 us  [shards(): lax.all_to_all(jnp.stack([key_weight] * lax.axis_size(('sec', 'dp'))), ('...]
    all_gather x1, waiting for transfers between devices: 53.2 us -> 26.3 us  [shards(): lax.all_gather(value_weight, ('sec', 'dp'), axis=0, tiled=True)]
    all_to_all x0 -> x1, starting transfers between devices: none -> 8.33 us  [shards(): lax.all_to_all(jnp.stack([key_weight] * lax.axis_size(('sec', 'dp'))), ('...]
    unnamed x7 -> x6, waiting for transfers between devices: 168 us -> 167 us
    unnamed x24 -> x28, local copies, waits for them, and re-layouts: 18.9 us -> 18.9 us
  transfers between devices with their start and end apart: 11 -> 11, of which waited for: 7 -> 7; matrix products, arithmetic and copies ran while one was open for 7% -> 8% of each run, Pallas kernels for 0% -> 0%
where the time goes in v1:
time: 590 us; the launch traced here: 589 us
  waiting for transfers between devices  439 us (74%)
  matrix products  45.6 us (8%)
  other arithmetic  33.9 us (6%)
  local copies, waits for them, and re-layouts  33.7 us (6%)
  starting transfers between devices  22.2 us (4%)
  between operations  14.2 us (2%)
    unnamed x6, waiting for transfers between devices  167 us
    psum x1, waiting for transfers between devices, shards(): lax.psum(partial_value.astype(jnp.bfloat16), 'tensor').astype(jnp.float32)  111 us
    all_gather x1, waiting for transfers between devices, shards(): lax.all_gather(query_weight, ('sec', 'dp'), axis=0, tiled=True)  56.7 us
    all_gather x1, waiting for transfers between devices, shards(): lax.all_gather(out_weight, ('sec', 'dp'), axis=0, tiled=True)  41.6 us
    all_to_all x1, waiting for transfers between devices, shards(): lax.all_to_all(jnp.stack([key_weight] * lax.axis_size(('sec', 'dp'))), ('...  31.8 us
    all_gather x1, waiting for transfers between devices, shards(): lax.all_gather(value_weight, ('sec', 'dp'), axis=0, tiled=True)  26.3 us
    unnamed x28, local copies, waits for them, and re-layouts  18.9 us
    ppermute x4, starting transfers between devices, from_behind(): return lax.ppermute(x, axis, pairs)  12.2 us
  transfers between devices with their start and end apart: 11, of which 7 were waited for; matrix products, arithmetic and copies ran while one was open for 8% of the time, Pallas kernels for 0%

profile of v1, /device:TPU:2, one launch (start us, length us, event | category | flops | bytes accessed | tf_op | source)
XLA Modules:
  0.0 588.5 jit_solution(10052636917179736601)
XLA Ops:
  7.2 0.7 all-gather.4.cloned.1.call-update
  7.9 0.7 all-gather.6.cloned.1.call-update
  8.7 0.7 all-gather.8.cloned.1.call-update
  9.4 2.6 stack.2
  12.0 8.3 %all-to-all-start = ((bf16[32,168,256]{2,1,0:T(8,128)(2,1)}), bf16[32,168,256]{2,1,0:T(8,128)(2,1)S(1)}, u32[]{:S(2)}, u32[]{:S(2)}) async-start(bf16[32,168,256]{2,1,0:T(8,128)(2,1)} %stack.2), calls=%async_computation | async-start | bytes 5505024 | tf_op jit(solution)/shard_map/all_to_all | solution.py:73
  20.4 3.8 fusion.9
  24.2 1.8 broadcast_multiply_fusion
  26.0 1.2 compare_and_fusion
  27.2 31.8 %all-to-all-done = bf16[32,168,256]{2,1,0:T(8,128)(2,1)S(1)} async-done(((bf16[32,168,256]{2,1,0:T(8,128)(2,1)}), bf16[32,168,256]{2,1,0:T(8,128)(2,1)S(1)}, u32[]{:S(2)}, u32[]{:S(2)}) %all-to-all-start) | async-done | bytes 2752544 | tf_op jit(solution)/shard_map/all_to_all | solution.py:73
  59.0 4.6 fusion.50
  63.6 1.2 fusion.66
  64.8 1.3 collective-permute-start.3
  66.1 4.7 collective-permute-start.2
  70.8 26.3 %all-gather.4.cloned.1.call-done = bf16[5376,256]{1,0:T(8,128)(2,1)} async-done(((bf16[168,256]{1,0:T(8,128)(2,1)}), bf16[5376,256]{1,0:T(8,128)(2,1)}) %all-gather.4.cloned.1.call-update) | async-done | bytes 2752528 | tf_op jit(solution)/shard_map/all_gather | solution.py:78
  97.1 5.1 fusion.53
  102.2 2.1 collective-permute-start.1
  104.3 4.0 collective-permute-start
  108.4 56.7 %all-gather.6.cloned.1.call-done = bf16[5376,512]{1,0:T(8,128)(2,1)} async-done(((bf16[168,512]{1,0:T(8,128)(2,1)}), bf16[5376,512]{1,0:T(8,128)(2,1)}) %all-gather.6.cloned.1.call-update) | async-done | bytes 5505040 | tf_op jit(solution)/shard_map/all_gather | solution.py:71
  165.1 8.4 %copy.30 = bf16[512,5376]{1,0:T(8,128)(2,1)} copy(bf16[512,5376]{0,1:T(8,128)(2,1)} %bitcast.136) | data formatting | bytes 11010048 | tf_op jit(solution)/shard_map/dot_general | solution.py:94
  173.5 7.0 %fusion.24 = f32[512,2,256]{0,2,1:T(8,128)S(1)} fusion(bf16[2,256,5376]{2,1,0:T(8,128)(2,1)} %bitcast.137, bf16[1,512,5376]{2,1,0:T(8,128)(2,1)} %param.8, f32[5376]{0:T(1024)S(1)} %copy-done.7, f32[512]{0:T(512)S(1)} %add_rsqrt_fusion.1), kind=kOutput, calls=%fused_computation.37 | convolution fusion | flops 2829582336 | bytes 12082176 | tf_op jit(solution)/shard_map/dot_general | solution.py:94
  180.5 0.2 subtract_convert_fusion.1
  180.7 1.4 fusion.31
  182.2 1.5 fusion.21
  183.7 1.1 copy-done.2
  184.8 2.3 fusion.47
  187.1 41.6 %all-gather.8.cloned.1.call-done = bf16[5376,512]{1,0:T(8,128)(2,1)} async-done(((bf16[168,512]{1,0:T(8,128)(2,1)}), bf16[5376,512]{1,0:T(8,128)(2,1)}) %all-gather.8.cloned.1.call-update) | async-done | bytes 5505040 | tf_op jit(solution)/shard_map/all_gather | solution.py:79
  228.7 7.4 %convolution_convert_fusion.2 = bf16[512,5376]{1,0:T(8,128)(2,1)} fusion(bf16[512,512]{0,1:T(8,128)(2,1)S(1)} %bitcast.142, bf16[5376,512]{1,0:T(8,128)(2,1)} %all-gather.8.cloned.1.call-done), kind=kOutput, calls=%fused_computation.26 | convolution fusion | flops 2821324800 | bytes 11534336 | tf_op jit(solution)/shard_map/te,de->td/dot_general | solution.py:134
  236.2 1.4 collective-permute-start.4
  237.7 111.0 %all-reduce.2.cloned.1.call-done = bf16[512,5376]{1,0:T(8,128)(2,1)} async-done(((bf16[512,5376]{1,0:T(8,128)(2,1)}), bf16[512,5376]{1,0:T(8,128)(2,1)}) %all-reduce.2.cloned.1.call-update) | async-done | bytes 5505040 | tf_op jit(solution)/shard_map/psum | solution.py:137
  348.6 3.9 fusion.15
  352.5 4.9 collective-permute-done.4
  357.4 7.1 %fusion.16 = (f32[512]{0:T(512)S(1)}, bf16[512,5376]{1,0:T(8,128)(2,1)S(1)}) fusion(bf16[512,5376]{1,0:T(8,128)(2,1)S(1)} %copy-done, bf16[512,5376]{1,0:T(8,128)(2,1)} %collective-permute-done.4, f32[5376]{0:T(1024)S(1)} %broadcast_multiply_fusion.1, f32[5376]{0:T(1024)S(1)} %copy-done.6, f32[512]{0:T(512)S(1)} %add_rsqrt_fusion, bf16[1,512,5376]{2,1,0:T(8,128)(2,1)} %param.8), kind=kLoop, calls=%fused_computation.21 | loop fusion | flops 33029632 | bytes 22067200 | tf_op jit(solution)/shard_map/reduce_sum | solution.py:142
  364.5 7.8 %fusion.8 = bf16[512,5376]{1,0:T(8,128)(2,1)S(1)} fusion(bf16[512,5376]{1,0:T(8,128)(2,1)S(1)} %copy-done, bf16[512,5376]{1,0:T(8,128)(2,1)} %collective-permute-done.4, bf16[512,5376]{1,0:T(8,128)(2,1)S(1)} %get-tuple-element.13, f32[512]{0:T(512)S(1)} %broadcast_multiply_fusion.2, f32[5376]{0:T(1024)S(1)} %broadcast_multiply_fusion.1, f32[512]{0:T(512)S(1)} %add_rsqrt_fusion), kind=kLoop, calls=%fused_computation.13 | loop fusion | flops 33030144 | bytes 22045696 | tf_op jit(solution)/shard_map/convert_element_type | solution.py:145
  372.4 3.5 convolution_convert_fusion
  375.8 5.8 convolution_convert_fusion.3
  381.6 2.3 fusion.17
  384.0 2.7 fusion.44
  386.7 0.2 subtract_convert_fusion
  387.0 3.6 convolution_convert_fusion.1
  390.6 5.1 pad_maximum_fusion
  395.7 14.7 %copy.48 = bf16[5376,1024]{1,0:T(8,128)(2,1)} copy(bf16[5376,1024]{0,1:T(8,128)(2,1)} %pad_maximum_fusion) | data formatting | bytes 22020096
  410.4 2.3 constant_dynamic-slice_fusion
  412.7 1.5 copy.35
  414.2 164.7 %reduce-scatter.4.cloned.1.call-done = bf16[168,1024]{1,0:T(8,128)(2,1)} async-done(((bf16[5376,1024]{1,0:T(8,128)(2,1)}), bf16[168,1024]{1,0:T(8,128)(2,1)}) %reduce-scatter.4.cloned.1.call-update) | async-done | bytes 344080
  578.9 1.2 copy.49
  580.1 0.1 fusion.83
  580.2 0.9 copy.39
  581.1 0.9 copy.38
  (47 shorter events, 0.4 us)
Async XLA Ops:
  7.2 89.9 %all-gather.4.cloned.1.call-start = ((), (), s32[]{:S(2)}) async-start(), calls=%async_computation.2 | async-start | bytes 2838528 | tf_op jit(solution)/shard_map/all_gather | solution.py:78
  7.9 157.2 %all-gather.6.cloned.1.call-start = ((), (), s32[]{:S(2)}) async-start(), calls=%async_computation.3 | async-start | bytes 5677056 | tf_op jit(solution)/shard_map/all_gather | solution.py:71
  8.6 220.1 %all-gather.8.cloned.1.call-start = ((), (), s32[]{:S(2)}) async-start(), calls=%async_computation.4 | async-start | bytes 5677056 | tf_op jit(solution)/shard_map/all_gather | solution.py:79
  12.0 47.1 %all-to-all-start = ((bf16[32,168,256]{2,1,0:T(8,128)(2,1)}), bf16[32,168,256]{2,1,0:T(8,128)(2,1)S(1)}, u32[]{:S(2)}, u32[]{:S(2)}) async-start(bf16[32,168,256]{2,1,0:T(8,128)(2,1)} %stack.2), calls=%async_computation | async-start | bytes 5505024 | tf_op jit(solution)/shard_map/all_to_all | solution.py:73
  20.3 328.3 %all-reduce.2.cloned.1.call-start = ((), (), s32[]{:S(2)}) async-start(), calls=%async_computation.5 | async-start | bytes 11010048 | tf_op jit(solution)/shard_map/psum | solution.py:137
  64.8 115.9 %collective-permute-start.3 = (bf16[512,256]{0,1:T(8,128)(2,1)S(1)}, bf16[512,256]{0,1:T(8,128)(2,1)S(1)}, u32[]{:S(2)}, u32[]{:S(2)}) collective-permute-start(bf16[512,256]{0,1:T(8,128)(2,1)S(1)} %maximum_bitcast_fusion.6), channel_id=1, source_target_pairs={{0,4},{4,8},{8,12},{12,16},{16,20},{20,24},{24,28},{28,32},{32,36}... | collective-permute-start | bytes 786440 | tf_op jit(solution)/shard_map/ppermute | solution.py:29
  66.1 114.6 %collective-permute-start.2 = (bf16[512,256]{0,1:T(8,128)(2,1)S(1)}, bf16[512,256]{0,1:T(8,128)(2,1)S(1)}, u32[]{:S(2)}, u32[]{:S(2)}) collective-permute-start(bf16[512,256]{0,1:T(8,128)(2,1)S(1)} %maximum_bitcast_fusion.6), channel_id=1, source_target_pairs={{0,8},{4,12},{8,16},{12,20},{16,24},{20,28},{24,32},{28,36},{32,40... | collective-permute-start | bytes 786440 | tf_op jit(solution)/shard_map/ppermute | solution.py:29
  102.2 71.3 %copy-start.7 = (f32[5376]{0:T(1024)S(1)}, f32[5376]{0:T(1024)}, u32[]{:S(2)}) copy-start(f32[5376]{0:T(1024)} %param.10) | copy-start | bytes 64516
  102.2 81.5 %collective-permute-start.1 = (bf16[512,256]{1,0:T(8,128)(2,1)S(1)}, bf16[512,256]{1,0:T(8,128)(2,1)S(1)}, u32[]{:S(2)}, u32[]{:S(2)}) collective-permute-start(bf16[512,256]{1,0:T(8,128)(2,1)S(1)} %fusion.53), channel_id=1, source_target_pairs={{0,4},{4,8},{8,12},{12,16},{16,20},{20,24},{24,28},{28,32},{32,36}... | collective-permute-start | bytes 786440 | tf_op jit(solution)/shard_map/ppermute | solution.py:29
  104.3 79.3 %collective-permute-start = (bf16[512,256]{1,0:T(8,128)(2,1)S(1)}, bf16[512,256]{1,0:T(8,128)(2,1)S(1)}, u32[]{:S(2)}, u32[]{:S(2)}) collective-permute-start(bf16[512,256]{1,0:T(8,128)(2,1)S(1)} %fusion.53), channel_id=1, source_target_pairs={{0,8},{4,12},{8,16},{12,20},{16,24},{20,28},{24,32},{28,36},{32,40... | collective-permute-start | bytes 786440 | tf_op jit(solution)/shard_map/ppermute | solution.py:29
  173.5 7.0 %copy-start.3 = (f32[512,128]{0,1:T(8,128)S(1)}, f32[512,128]{0,1:T(8,128)}, u32[]{:S(2)}) copy-start(f32[512,128]{0,1:T(8,128)} %get-tuple-element.24) | copy-start | bytes 786436
  173.5 7.0 %copy-start.5 = (f32[512,128]{0,1:T(8,128)S(1)}, f32[512,128]{0,1:T(8,128)}, u32[]{:S(2)}) copy-start(f32[512,128]{0,1:T(8,128)} %get-tuple-element.23) | copy-start | bytes 786436
  182.1 2.7 copy-start.2
  228.7 9.0 %copy-start.6 = (f32[5376]{0:T(1024)S(1)}, f32[5376]{0:T(1024)}, u32[]{:S(2)}) copy-start(f32[5376]{0:T(1024)} %param.11) | copy-start | bytes 64516
  236.2 342.7 %reduce-scatter.4.cloned.1.call-start = ((), (), s32[]{:S(2)}) async-start(), calls=%async_computation.6 | async-start | bytes 11354112
  236.2 121.2 %collective-permute-start.4 = (bf16[512,5376]{1,0:T(8,128)(2,1)}, bf16[512,5376]{1,0:T(8,128)(2,1)}, u32[]{:S(2)}, u32[]{:S(2)}) collective-permute-start(bf16[512,5376]{1,0:T(8,128)(2,1)} %bitcast.141), channel_id=1, source_target_pairs={{0,64},{64,0},{1,65},{65,1},{2,66},{66,2},{3,67},{67,3},{4,68},{68... | collective-permute-start | bytes 16515080 | tf_op jit(solution)/shard_map/ppermute | solution.py:23
  348.6 8.8 %copy-start = (bf16[512,5376]{1,0:T(8,128)(2,1)S(1)}, bf16[512,5376]{1,0:T(8,128)(2,1)}, u32[]{:S(2)}) copy-start(bf16[512,5376]{1,0:T(8,128)(2,1)} %all-reduce.2.cloned.1.call-done) | copy-start | bytes 16515076
  364.5 7.9 %copy-start.1 = (bf16[512,5376]{1,0:T(8,128)(2,1)}, bf16[512,5376]{1,0:T(8,128)(2,1)S(1)}, u32[]{:S(2)}) copy-start(bf16[512,5376]{1,0:T(8,128)(2,1)S(1)} %get-tuple-element.13) | copy-start | bytes 16515076
  372.4 9.2 %slice-start.2 = ((s8[6291456]{0:T(1024)(128)(4,1)}), s8[4194304]{0:T(1024)(128)(4,1)S(1)}, s32[]{:S(2)}) async-start(s8[6291456]{0:T(1024)(128)(4,1)} %bitcast.134), calls=%async_computation.9 | async-start | bytes 8388608
  375.8 5.8 slice-start.3
  381.6 5.3 slice-start
  384.0 2.7 copy-start.4
  384.0 3.0 slice-start.1
Sparse Core Ops, SparseCore 0:
  9.7 87.3 all-gather.3
  98.8 66.2 all-gather.5
  166.8 61.8 all-gather.7
  236.3 112.3 all-reduce.1
  410.5 168.3 reduce-scatter.3
